TPU v7x, 32 devices: a whole 2x2x4 slice. The times are simulated.
32 devices in a mesh: shard: 4 (over y, x), context: 4 (over z), tensor: 2 (over core).
Axes of the slice: x: 2, y: 2, z: 4, core: 2. Of those that a mesh axis runs over, the one named last changes fastest.
Arguments:
- tokens: bfloat16 [12, 1024, 768], P('shard', 'context'), may hold values from -6 to 6
- lengths: int32 [12], P('shard'), may hold values from 256 to 1024, as said below
- cotangent: bfloat16 [12, 1024, 768], P('shard', 'context'), may hold values from -6 to 6
- norm_attn: bfloat16 [768], P('shard'), may hold values from 0.099609375 to 1.8984375
- w_query: bfloat16 [768, 768], P('shard', 'tensor'), may hold values from -0.02734375 to 0.02734375
- w_key: bfloat16 [768, 768], P('shard', 'tensor'), may hold values from -0.21875 to 0.21875
- w_value: bfloat16 [768, 768], P('shard', 'tensor'), may hold values from -0.21875 to 0.21875
- w_attn_out: bfloat16 [768, 768], P('tensor', 'shard'), may hold values from -1.25 to 1.25
- bias_table: bfloat16 [32, 12], P('shard', 'tensor'), may hold values from -4 to 4
- norm_ffn: bfloat16 [768], P('shard'), may hold values from 0.099609375 to 1.8984375
- w_ffn_in: bfloat16 [768, 3072], P('shard', 'tensor'), may hold values from -0.21875 to 0.21875
- w_ffn_out: bfloat16 [3072, 768], P('tensor', 'shard'), may hold values from -0.109375 to 0.109375
Outputs:
- out: bfloat16 [12, 1024, 768], P('shard', 'context')
- grad_tokens: float32 [12, 1024, 768], P('shard', 'context')
- grad_norm_attn: float32 [768], P('shard')
- grad_w_query: float32 [768, 768], P('shard', 'tensor')
- grad_w_key: float32 [768, 768], P('shard', 'tensor')
- gradient_value_weight: float32 [768, 768], P('shard', 'tensor')
- grad_w_attn_out: float32 [768, 768], P('tensor', 'shard')
- gradient_bias_lookup: float32 [32, 12], P('shard', 'tensor')
- grad_norm_ffn: float32 [768], P('shard')
- grad_w_ffn_in: float32 [768, 3072], P('shard', 'tensor')
- grad_w_ffn_out: float32 [3072, 768], P('tensor', 'shard')
Inputs may be any that keep to these rules, and one draw needn't show every extreme that they name: A slot's valid tokens are its first lengths[s] positions. Some slot holds exactly 1024 and some exactly 256.
All inputs are finite; a program needn't handle non-finite values.
Results may differ from a plain program's by a relative error of at most 0.028.
Values may be sent and summed in bfloat16 or wider, within the bound.
No kernel may reach another device: no remote copies, remote signals or barrier semaphores. Data moves between devices by JAX's collectives and lax.ppermute only.
A program may use at most 256 MiB of HBM per device.

v0:
```python
import jax
import jax.numpy as jnp
from jax import lax
from jax.sharding import PartitionSpec as P

NB = 32
L = 1024
MICRO = 3
boundaries = (12, 16, 23, 32, 46, 64, 91)
eps_norm = 1e-06
masked_score = -1000000000.0


def shortened(shard):
    return jax.tree.map(lambda a: a.astype(jnp.bfloat16) if a.dtype == jnp.float32 else a, shard)


def gelu_tanh(value):
    return (
        0.5
        * value
        * (1.0 + jnp.tanh(0.7978845608028654 * (value + 0.044715 * value * value * value)))
    )


def bucket_of(query_pos, key_pos):
    relative = key_pos[None, :] - query_pos[:, None]
    distance = jnp.abs(relative)
    bucket_idx = 16 * (relative > 0).astype(jnp.int32) + jnp.minimum(distance, 8)
    for boundary in boundaries:
        bucket_idx = bucket_idx + (distance >= boundary).astype(jnp.int32)
    return bucket_idx


def matrix_product(left, right, form):
    return jnp.einsum(form, left, right, preferred_element_type=jnp.float32)


def normalize(stream, gain):
    scale_row = lax.rsqrt(jnp.mean(stream * stream, axis=-1, keepdims=True) + eps_norm)
    return (scale_row, (stream * scale_row * gain.astype(jnp.float32)).astype(jnp.bfloat16))


def norm_back(stream, scale_row, gain, grad_normed):
    scaled = gain.astype(jnp.float32) * grad_normed
    grad_gain = jnp.sum(stream * scale_row * grad_normed, axis=0)
    cubed = scale_row * scale_row * scale_row
    grad_stream = scale_row * scaled - stream * cubed * jnp.mean(
        stream * scaled, axis=-1, keepdims=True
    )
    return (grad_stream, grad_gain)


def fetch_forward(shards):
    return (
        lax.all_gather(shards[0], "shard", axis=0, tiled=True),
        lax.all_gather(shards[1], "shard", axis=0, tiled=True),
        lax.all_gather(shards[2], "shard", axis=0, tiled=True),
        lax.all_gather(shards[3], "shard", axis=0, tiled=True),
        lax.all_gather(shards[4], "shard", axis=1, tiled=True),
        lax.all_gather(shards[5], "shard", axis=0, tiled=True),
        lax.all_gather(shards[6], "shard", axis=0, tiled=True),
        lax.all_gather(shards[7], "shard", axis=0, tiled=True),
        lax.all_gather(shards[8], "shard", axis=1, tiled=True),
    )


def fetch_backward(shards):
    return (
        lax.all_gather(shards[0], "shard", axis=0, tiled=True),
        lax.all_gather(shards[1], "shard", axis=0, tiled=True),
        lax.all_gather(shards[2], "shard", axis=0, tiled=True),
        lax.all_gather(shards[3], "shard", axis=0, tiled=True),
        lax.all_gather(shards[4], "shard", axis=1, tiled=True),
        lax.all_gather(shards[5], "shard", axis=0, tiled=True),
        lax.all_gather(shards[6], "shard", axis=0, tiled=True),
        lax.all_gather(shards[7], "shard", axis=0, tiled=True),
        lax.all_gather(shards[8], "shard", axis=1, tiled=True),
    )


def forward_total(partial_sum):
    return lax.psum(partial_sum.astype(jnp.bfloat16), "tensor").astype(jnp.float32)


def backward_total(partial_sum):
    return lax.psum(partial_sum.astype(jnp.bfloat16), "tensor").astype(jnp.float32)


def masked_scores(query_heads, key_heads, head_bias_rows, key_valid):
    raw_scores = matrix_product(query_heads, key_heads, "sqhd,skhd->shqk") + head_bias_rows[None]
    return jnp.where(key_valid[:, None, None, :], raw_scores, masked_score)


def block_forward(stream, weight_arrays, head_bias_rows, key_valid):
    norm_attn, w_query, w_key, w_value, w_attn_out, bias_table, norm_ffn, w_ffn_in, w_ffn_out = (
        weight_arrays
    )
    slots_mb, total_len = key_valid.shape
    head_count = head_bias_rows.shape[0]
    inner_width = w_query.shape[1]
    head_dim = inner_width // head_count
    rows_local = stream.shape[0] // slots_mb
    normed_one = normalize(stream, norm_attn)[1]
    queries = matrix_product(normed_one, w_query, "rd,dc->rc").astype(jnp.bfloat16)
    keys_local = matrix_product(normed_one, w_key, "rd,dc->rc").astype(jnp.bfloat16)
    values_local = matrix_product(normed_one, w_value, "rd,dc->rc").astype(jnp.bfloat16)
    keys_full, values_full = (
        lax.all_gather(
            keys_local.reshape(slots_mb, rows_local, inner_width), "context", axis=1, tiled=True
        ),
        lax.all_gather(
            values_local.reshape(slots_mb, rows_local, inner_width), "context", axis=1, tiled=True
        ),
    )
    query_heads = queries.reshape(slots_mb, rows_local, head_count, head_dim)
    key_heads = keys_full.reshape(slots_mb, total_len, head_count, head_dim)
    value_heads = values_full.reshape(slots_mb, total_len, head_count, head_dim)
    scores = masked_scores(query_heads, key_heads, head_bias_rows, key_valid)
    row_max = jnp.max(scores, axis=-1, keepdims=True)
    shifted_exp = jnp.exp(scores - row_max)
    row_total = jnp.sum(shifted_exp, axis=-1, keepdims=True)
    probs_low = (shifted_exp / row_total).astype(jnp.bfloat16)
    log_total = row_max + jnp.log(row_total)
    context = (
        matrix_product(probs_low, value_heads, "shqk,skhd->sqhd")
        .astype(jnp.bfloat16)
        .reshape(-1, inner_width)
    )
    middle = stream + forward_total(matrix_product(context, w_attn_out, "rc,cd->rd"))
    normed_two = normalize(middle, norm_ffn)[1]
    pre_act = matrix_product(normed_two, w_ffn_in, "rd,df->rf")
    hidden_state = gelu_tanh(pre_act).astype(jnp.bfloat16)
    result = middle + forward_total(matrix_product(hidden_state, w_ffn_out, "rf,fd->rd"))
    return (
        result,
        (
            stream,
            middle,
            query_heads,
            key_heads,
            value_heads,
            log_total,
            context,
            pre_act,
            hidden_state,
        ),
    )


def block_backward(
    saved_state, grad_out, weight_arrays, head_bias_rows, bucket_indicator, key_valid
):
    norm_attn, w_query, w_key, w_value, w_attn_out, bias_table, norm_ffn, w_ffn_in, w_ffn_out = (
        weight_arrays
    )
    (
        stream,
        middle,
        query_heads,
        key_heads,
        value_heads,
        log_total,
        context,
        pre_act,
        hidden_state,
    ) = saved_state
    slots_mb, rows_local, head_count, head_dim = query_heads.shape
    total_len = key_heads.shape[1]
    inner_width = head_count * head_dim
    grad_ffn = grad_out.astype(jnp.bfloat16)
    grad_w_ffn_out = matrix_product(hidden_state, grad_ffn, "rf,rd->fd")
    grad_hidden = matrix_product(grad_ffn, w_ffn_out, "rd,fd->rf")
    unused_value, gelu_pull = jax.vjp(gelu_tanh, pre_act)
    grad_pre = gelu_pull(grad_hidden)[0].astype(jnp.bfloat16)
    scale_two, normed_two = normalize(middle, norm_ffn)
    grad_w_ffn_in = matrix_product(normed_two, grad_pre, "rd,rf->df")
    grad_normed_two = backward_total(matrix_product(grad_pre, w_ffn_in, "rf,df->rd"))
    grad_middle_norm, grad_norm_ffn = norm_back(middle, scale_two, norm_ffn, grad_normed_two)
    grad_middle = grad_out + grad_middle_norm
    grad_attn = grad_middle.astype(jnp.bfloat16)
    grad_w_attn_out = matrix_product(context, grad_attn, "rc,rd->cd")
    grad_context = matrix_product(grad_attn, w_attn_out, "rd,cd->rc").astype(jnp.bfloat16)
    grad_context = grad_context.reshape(slots_mb, rows_local, head_count, head_dim)
    scores = masked_scores(query_heads, key_heads, head_bias_rows, key_valid)
    attn_probs = jnp.exp(scores - log_total)
    probs_low = attn_probs.astype(jnp.bfloat16)
    grad_probs = matrix_product(grad_context, value_heads, "sqhd,skhd->shqk")
    row_inner = jnp.sum(attn_probs * grad_probs, axis=-1, keepdims=True)
    gradient_score_matrix = (attn_probs * (grad_probs - row_inner)).astype(jnp.bfloat16)
    gradient_bias_lookup = matrix_product(bucket_indicator, gradient_score_matrix, "gfn,eofn->go")
    grad_queries = (
        matrix_product(gradient_score_matrix, key_heads, "shqk,skhd->sqhd")
        .astype(jnp.bfloat16)
        .reshape(-1, inner_width)
    )
    key_part = matrix_product(gradient_score_matrix, query_heads, "shqk,sqhd->skhd").reshape(
        slots_mb, total_len, inner_width
    )
    value_part = matrix_product(probs_low, grad_context, "shqk,sqhd->skhd").reshape(
        slots_mb, total_len, inner_width
    )
    grad_keys, grad_values = (
        lax.psum_scatter(
            key_part.astype(jnp.bfloat16), "context", scatter_dimension=1, tiled=True
        ).astype(jnp.float32),
        lax.psum_scatter(
            value_part.astype(jnp.bfloat16), "context", scatter_dimension=1, tiled=True
        ).astype(jnp.float32),
    )
    grad_keys = grad_keys.astype(jnp.bfloat16).reshape(-1, inner_width)
    grad_values = grad_values.astype(jnp.bfloat16).reshape(-1, inner_width)
    scale_one, normed_one = normalize(stream, norm_attn)
    grad_w_query = matrix_product(normed_one, grad_queries, "rd,rc->dc")
    grad_w_key = matrix_product(normed_one, grad_keys, "rd,rc->dc")
    gradient_value_weight = matrix_product(normed_one, grad_values, "rd,rc->dc")
    normed_partial = (
        matrix_product(grad_queries, w_query, "rc,dc->rd")
        + matrix_product(grad_keys, w_key, "rc,dc->rd")
        + matrix_product(grad_values, w_value, "rc,dc->rd")
    )
    grad_normed_one = backward_total(normed_partial)
    grad_stream_norm, grad_norm_attn = norm_back(stream, scale_one, norm_attn, grad_normed_one)
    increments = (
        grad_norm_attn,
        grad_w_query,
        grad_w_key,
        gradient_value_weight,
        grad_w_attn_out,
        gradient_bias_lookup,
        grad_norm_ffn,
        grad_w_ffn_in,
        grad_w_ffn_out,
    )
    return (grad_middle + grad_stream_norm, increments)


def body(
    tokens,
    lengths,
    cotangent,
    norm_attn,
    w_query,
    w_key,
    w_value,
    w_attn_out,
    bias_table,
    norm_ffn,
    w_ffn_in,
    w_ffn_out,
):
    local_slots, rows_local, model_width = tokens.shape
    slots_mb = local_slots // MICRO
    shards = (
        norm_attn,
        w_query,
        w_key,
        w_value,
        w_attn_out,
        bias_table,
        norm_ffn,
        w_ffn_in,
        w_ffn_out,
    )
    query_pos = lax.axis_index("context") * rows_local + jnp.arange(rows_local, dtype=jnp.int32)
    key_pos = jnp.arange(L, dtype=jnp.int32)
    bucket_idx = bucket_of(query_pos, key_pos)
    bucket_indicator = (bucket_idx[None] == jnp.arange(NB, dtype=jnp.int32)[:, None, None]).astype(
        jnp.bfloat16
    )
    outputs = []
    grad_inputs = []
    totals = None
    for batch_idx in range(MICRO):
        first_slot = batch_idx * slots_mb
        lens_micro = lengths[first_slot : first_slot + slots_mb]
        key_valid = key_pos[None, :] < lens_micro[:, None]
        row_valid = (query_pos[None, :] < lens_micro[:, None]).reshape(-1, 1)
        stream = (
            tokens[first_slot : first_slot + slots_mb].astype(jnp.float32).reshape(-1, model_width)
        )
        records = []
        for layer_idx in range(2):
            weight_arrays = fetch_forward(shards)
            head_bias_rows = matrix_product(bucket_indicator, weight_arrays[5], "ves,vi->ies")
            stream, saved_state = block_forward(stream, weight_arrays, head_bias_rows, key_valid)
            records.append((saved_state, head_bias_rows))
        outputs.append(
            jnp.where(row_valid, stream, 0.0)
            .astype(jnp.bfloat16)
            .reshape(slots_mb, rows_local, model_width)
        )
        grad_stream = (
            cotangent[first_slot : first_slot + slots_mb]
            .astype(jnp.float32)
            .reshape(-1, model_width)
        )
        grad_stream = jnp.where(row_valid, grad_stream, 0.0)
        for layer_idx in (1, 0):
            weight_arrays = fetch_backward(shards)
            saved_state, head_bias_rows = records[layer_idx]
            grad_stream, increments = block_backward(
                saved_state, grad_stream, weight_arrays, head_bias_rows, bucket_indicator, key_valid
            )
            if totals is None:
                totals = increments
            else:
                totals = jax.tree.map(jnp.add, totals, increments)
        grad_inputs.append(grad_stream.reshape(slots_mb, rows_local, model_width))
    reduced = (
        lax.psum_scatter(
            totals[0].astype(jnp.bfloat16), "shard", scatter_dimension=0, tiled=True
        ).astype(jnp.float32),
        lax.psum_scatter(
            totals[1].astype(jnp.bfloat16), "shard", scatter_dimension=0, tiled=True
        ).astype(jnp.float32),
        lax.psum_scatter(
            totals[2].astype(jnp.bfloat16), "shard", scatter_dimension=0, tiled=True
        ).astype(jnp.float32),
        lax.psum_scatter(
            totals[3].astype(jnp.bfloat16), "shard", scatter_dimension=0, tiled=True
        ).astype(jnp.float32),
        lax.psum_scatter(
            totals[4].astype(jnp.bfloat16), "shard", scatter_dimension=1, tiled=True
        ).astype(jnp.float32),
        lax.psum_scatter(
            totals[5].astype(jnp.bfloat16), "shard", scatter_dimension=0, tiled=True
        ).astype(jnp.float32),
        lax.psum_scatter(
            totals[6].astype(jnp.bfloat16), "shard", scatter_dimension=0, tiled=True
        ).astype(jnp.float32),
        lax.psum_scatter(
            totals[7].astype(jnp.bfloat16), "shard", scatter_dimension=0, tiled=True
        ).astype(jnp.float32),
        lax.psum_scatter(
            totals[8].astype(jnp.bfloat16), "shard", scatter_dimension=1, tiled=True
        ).astype(jnp.float32),
    )
    summed = jax.tree.map(
        lambda part: part.astype(jnp.float32), lax.psum(shortened(reduced), "context")
    )
    return (jnp.concatenate(outputs, axis=0), jnp.concatenate(grad_inputs, axis=0)) + tuple(summed)


def solution(mesh):
    return jax.shard_map(
        body,
        mesh=mesh,
        in_specs=(
            P("shard", "context", None),
            P("shard"),
            P("shard", "context", None),
            P("shard"),
            P("shard", "tensor"),
            P("shard", "tensor"),
            P("shard", "tensor"),
            P("tensor", "shard"),
            P("shard", "tensor"),
            P("shard"),
            P("shard", "tensor"),
            P("tensor", "shard"),
        ),
        out_specs=(
            P("shard", "context", None),
            P("shard", "context", None),
            P("shard"),
            P("shard", "tensor"),
            P("shard", "tensor"),
            P("shard", "tensor"),
            P("tensor", "shard"),
            P("shard", "tensor"),
            P("shard"),
            P("shard", "tensor"),
            P("tensor", "shard"),
        ),
        check_vma=False,
    )
```

profile of v0, /device:TPU:0, one launch (start us, length us, event | category | flops | bytes accessed | tf_op | source)
XLA Modules:
  0.0 1300.5 jit_solution(5848449888905691119)
XLA Ops:
  8.1 12.4 all_gather.43
  24.1 9.5 all-reduce.8
  33.6 9.8 all_gather.45
  47.6 9.8 all_gather.46
  62.4 17.5 %all-gather.8 = bf16[1024,384]{1,0:T(8,128)(2,1)} all-gather(bf16[256,384]{1,0:T(8,128)(2,1)S(1)} %convolution_convert_fusion.41), channel_id=10, replica_groups=mesh['shard'=4,'context'=4,'tensor'=2] {'context'}, dimensions={0}, use_global_device_ids=true | all-gather | bytes 983040 | tf_op jit(solution)/shard_map/all_gather | solution.py:112
  92.9 16.3 %all-gather.9 = bf16[1024,384]{1,0:T(8,128)(2,1)} all-gather(bf16[256,384]{1,0:T(8,128)(2,1)S(1)} %convolution_convert_fusion.39), channel_id=11, replica_groups=mesh['shard'=4,'context'=4,'tensor'=2] {'context'}, dimensions={0}, use_global_device_ids=true | all-gather | bytes 983040 | tf_op jit(solution)/shard_map/all_gather | solution.py:109
  112.7 10.3 all_gather.49
  123.0 20.1 %all-gather = bf16[1024,384]{1,0:T(8,128)(2,1)} all-gather(bf16[256,384]{1,0:T(8,128)(2,1)} %convolution_convert_fusion.53), channel_id=2, replica_groups=mesh['shard'=4,'context'=4,'tensor'=2] {'context'}, dimensions={0}, use_global_device_ids=true | all-gather | bytes 983040 | tf_op jit(solution)/shard_map/all_gather | solution.py:112
  147.1 16.8 %all-gather.1 = bf16[1024,384]{1,0:T(8,128)(2,1)} all-gather(bf16[256,384]{1,0:T(8,128)(2,1)} %convolution_convert_fusion.51), channel_id=3, replica_groups=mesh['shard'=4,'context'=4,'tensor'=2] {'context'}, dimensions={0}, use_global_device_ids=true | all-gather | bytes 983040 | tf_op jit(solution)/shard_map/all_gather | solution.py:109
  195.0 18.7 %all-gather.4 = bf16[1024,384]{1,0:T(8,128)(2,1)} all-gather(bf16[256,384]{1,0:T(8,128)(2,1)S(1)} %copy-done.212), channel_id=6, replica_groups=mesh['shard'=4,'context'=4,'tensor'=2] {'context'}, dimensions={0}, use_global_device_ids=true | all-gather | bytes 983040 | tf_op jit(solution)/shard_map/all_gather | solution.py:112
  217.8 16.8 %all-gather.5 = bf16[1024,384]{1,0:T(8,128)(2,1)} all-gather(bf16[256,384]{1,0:T(8,128)(2,1)} %convolution_convert_fusion.45), channel_id=7, replica_groups=mesh['shard'=4,'context'=4,'tensor'=2] {'context'}, dimensions={0}, use_global_device_ids=true | all-gather | bytes 983040 | tf_op jit(solution)/shard_map/all_gather | solution.py:109
  237.5 8.2 fusion.408
  254.2 16.7 %all-reduce.39.cloned.1.call-done = (bf16[256,768]{1,0:T(8,128)(2,1)}, bf16[256,768]{1,0:T(8,128)(2,1)}, bf16[256,768]{1,0:T(8,128)(2,1)}) async-done(((bf16[256,768]{1,0:T(8,128)(2,1)}, bf16[256,768]{1,0:T(8,128)(2,1)}, bf16[256,768]{1,0:T(8,128)(2,1)}), (bf16[256,768]{1,0:T(8,128)(2,1)}, bf16[256,768]{1,0:T(8,128)(2,1)}, bf16[256,768]{1,0:T(8,128)(2,1)})) %all-reduce.39.cloned.1.call-update) | async-done | bytes 1179664 | tf_op jit(solution)/shard_map/psum | solution.py:83
  274.4 16.3 %all-gather.15.cloned.1.call-done = bf16[768,1536]{1,0:T(8,128)(2,1)} async-done(((bf16[192,1536]{1,0:T(8,128)(2,1)}), bf16[768,1536]{1,0:T(8,128)(2,1)}) %all-gather.15.cloned.1.call-update) | async-done | bytes 2359312 | tf_op jit(solution)/shard_map/all_gather | solution.py:63
  296.7 33.2 %all-gather.17.cloned.1.call-done = bf16[1536,768]{0,1:T(8,128)(2,1)} async-done(((bf16[1536,192]{0,1:T(8,128)(2,1)}), bf16[1536,768]{0,1:T(8,128)(2,1)}) %all-gather.17.cloned.1.call-update) | async-done | bytes 2359312 | tf_op jit(solution)/shard_map/all_gather | solution.py:64
  339.8 20.0 %all-reduce.37.cloned.1.call-done = (bf16[256,768]{1,0:T(8,128)(2,1)}, bf16[256,768]{1,0:T(8,128)(2,1)}, bf16[256,768]{1,0:T(8,128)(2,1)}) async-done(((bf16[256,768]{1,0:T(8,128)(2,1)}, bf16[256,768]{1,0:T(8,128)(2,1)}, bf16[256,768]{1,0:T(8,128)(2,1)}), (bf16[256,768]{1,0:T(8,128)(2,1)}, bf16[256,768]{1,0:T(8,128)(2,1)}, bf16[256,768]{1,0:T(8,128)(2,1)})) %all-reduce.37.cloned.1.call-update) | async-done | bytes 1179664 | tf_op jit(solution)/shard_map/psum | solution.py:83
  373.3 19.8 %all-gather.10 = bf16[1024,384]{1,0:T(8,128)(2,1)S(1)} all-gather(bf16[256,384]{1,0:T(8,128)(2,1)S(1)} %convolution_convert_fusion.38), channel_id=12, replica_groups=mesh['shard'=4,'context'=4,'tensor'=2] {'context'}, dimensions={0}, use_global_device_ids=true | all-gather | bytes 983040 | tf_op jit(solution)/shard_map/all_gather | solution.py:112
  394.7 18.4 %all-gather.11 = bf16[1024,384]{1,0:T(8,128)(2,1)} all-gather(bf16[256,384]{1,0:T(8,128)(2,1)} %convolution_convert_fusion.36), channel_id=13, replica_groups=mesh['shard'=4,'context'=4,'tensor'=2] {'context'}, dimensions={0}, use_global_device_ids=true | all-gather | bytes 983040 | tf_op jit(solution)/shard_map/all_gather | solution.py:109
  414.6 8.2 fusion.409
  428.3 17.4 %all-gather.6 = bf16[1024,384]{1,0:T(8,128)(2,1)S(1)} all-gather(bf16[256,384]{1,0:T(8,128)(2,1)S(1)} %copy-done.189), channel_id=8, replica_groups=mesh['shard'=4,'context'=4,'tensor'=2] {'context'}, dimensions={0}, use_global_device_ids=true | all-gather | bytes 983040 | tf_op jit(solution)/shard_map/all_gather | solution.py:112
  447.3 18.3 %all-gather.7 = bf16[1024,384]{1,0:T(8,128)(2,1)} all-gather(bf16[256,384]{1,0:T(8,128)(2,1)} %convolution_convert_fusion.42), channel_id=9, replica_groups=mesh['shard'=4,'context'=4,'tensor'=2] {'context'}, dimensions={0}, use_global_device_ids=true | all-gather | bytes 983040 | tf_op jit(solution)/shard_map/all_gather | solution.py:109
  467.0 8.2 fusion.410
  480.8 17.2 %all-gather.2 = bf16[1024,384]{1,0:T(8,128)(2,1)S(1)} all-gather(bf16[256,384]{1,0:T(8,128)(2,1)S(1)} %copy-done.188), channel_id=4, replica_groups=mesh['shard'=4,'context'=4,'tensor'=2] {'context'}, dimensions={0}, use_global_device_ids=true | all-gather | bytes 983040 | tf_op jit(solution)/shard_map/all_gather | solution.py:112
  499.6 16.8 %all-gather.3 = bf16[1024,384]{1,0:T(8,128)(2,1)} all-gather(bf16[256,384]{1,0:T(8,128)(2,1)} %convolution_convert_fusion.48), channel_id=5, replica_groups=mesh['shard'=4,'context'=4,'tensor'=2] {'context'}, dimensions={0}, use_global_device_ids=true | all-gather | bytes 983040 | tf_op jit(solution)/shard_map/all_gather | solution.py:109
  517.8 8.2 fusion.411
  535.2 16.9 %all-reduce.35.cloned.1.call-done = (bf16[256,768]{1,0:T(8,128)(2,1)}, bf16[256,768]{1,0:T(8,128)(2,1)}, bf16[256,768]{1,0:T(8,128)(2,1)}) async-done(((bf16[256,768]{1,0:T(8,128)(2,1)}, bf16[256,768]{1,0:T(8,128)(2,1)}, bf16[256,768]{1,0:T(8,128)(2,1)}), (bf16[256,768]{1,0:T(8,128)(2,1)}, bf16[256,768]{1,0:T(8,128)(2,1)}, bf16[256,768]{1,0:T(8,128)(2,1)})) %all-reduce.35.cloned.1.call-update) | async-done | bytes 1179664 | tf_op jit(solution)/shard_map/psum | solution.py:83
  574.4 20.4 %all-reduce.33.cloned.1.call-done = (bf16[256,768]{1,0:T(8,128)(2,1)}, bf16[256,768]{1,0:T(8,128)(2,1)}, bf16[256,768]{1,0:T(8,128)(2,1)}) async-done(((bf16[256,768]{1,0:T(8,128)(2,1)}, bf16[256,768]{1,0:T(8,128)(2,1)}, bf16[256,768]{1,0:T(8,128)(2,1)}), (bf16[256,768]{1,0:T(8,128)(2,1)}, bf16[256,768]{1,0:T(8,128)(2,1)}, bf16[256,768]{1,0:T(8,128)(2,1)})) %all-reduce.33.cloned.1.call-update) | async-done | bytes 1179664 | tf_op jit(solution)/shard_map/psum | solution.py:87
  664.2 21.1 %reduce-scatter.19.cloned.1.call-done = bf16[1,256,384]{1,2,0:T(8,128)(2,1)} async-done(((bf16[1,1024,384]{1,2,0:T(8,128)(2,1)}), bf16[1,256,384]{1,2,0:T(8,128)(2,1)}) %reduce-scatter.19.cloned.1.call-update) | async-done | bytes 196624 | tf_op jit(solution)/shard_map/reduce_scatter | solution.py:204
  687.5 22.7 %reduce-scatter.21.cloned.1.call-done = bf16[1,256,384]{1,2,0:T(8,128)(2,1)} async-done(((bf16[1,1024,384]{1,2,0:T(8,128)(2,1)}), bf16[1,256,384]{1,2,0:T(8,128)(2,1)}) %reduce-scatter.21.cloned.1.call-update) | async-done | bytes 196624 | tf_op jit(solution)/shard_map/reduce_scatter | solution.py:207
  712.6 22.5 %reduce-scatter.27.cloned.1.call-done = bf16[1,256,384]{1,2,0:T(8,128)(2,1)} async-done(((bf16[1,1024,384]{1,2,0:T(8,128)(2,1)}), bf16[1,256,384]{1,2,0:T(8,128)(2,1)}) %reduce-scatter.27.cloned.1.call-update) | async-done | bytes 196624 | tf_op jit(solution)/shard_map/reduce_scatter | solution.py:204
  737.3 22.5 %reduce-scatter.29.cloned.1.call-done = bf16[1,256,384]{1,2,0:T(8,128)(2,1)} async-done(((bf16[1,1024,384]{1,2,0:T(8,128)(2,1)}), bf16[1,256,384]{1,2,0:T(8,128)(2,1)}) %reduce-scatter.29.cloned.1.call-update) | async-done | bytes 196624 | tf_op jit(solution)/shard_map/reduce_scatter | solution.py:207
  762.3 19.3 %all-reduce.31.cloned.1.call-done = (bf16[256,768]{1,0:T(8,128)(2,1)}, bf16[256,768]{1,0:T(8,128)(2,1)}, bf16[256,768]{1,0:T(8,128)(2,1)}) async-done(((bf16[256,768]{1,0:T(8,128)(2,1)}, bf16[256,768]{1,0:T(8,128)(2,1)}, bf16[256,768]{1,0:T(8,128)(2,1)}), (bf16[256,768]{1,0:T(8,128)(2,1)}, bf16[256,768]{1,0:T(8,128)(2,1)}, bf16[256,768]{1,0:T(8,128)(2,1)})) %all-reduce.31.cloned.1.call-update) | async-done | bytes 1179664 | tf_op jit(solution)/shard_map/psum | solution.py:87
  800.6 19.6 %all-reduce.29.cloned.1.call-done = (bf16[256,768]{1,0:T(8,128)(2,1)}, bf16[256,768]{1,0:T(8,128)(2,1)}, bf16[256,768]{1,0:T(8,128)(2,1)}) async-done(((bf16[256,768]{1,0:T(8,128)(2,1)}, bf16[256,768]{1,0:T(8,128)(2,1)}, bf16[256,768]{1,0:T(8,128)(2,1)}), (bf16[256,768]{1,0:T(8,128)(2,1)}, bf16[256,768]{1,0:T(8,128)(2,1)}, bf16[256,768]{1,0:T(8,128)(2,1)})) %all-reduce.29.cloned.1.call-update) | async-done | bytes 1179664 | tf_op jit(solution)/shard_map/psum | solution.py:87
  921.2 12.9 reduce-scatter.25.cloned.1.call-done
  937.3 21.4 %reduce-scatter.33.cloned.1.call-done = bf16[1,256,384]{1,2,0:T(8,128)(2,1)} async-done(((bf16[1,1024,384]{1,2,0:T(8,128)(2,1)}), bf16[1,256,384]{1,2,0:T(8,128)(2,1)}) %reduce-scatter.33.cloned.1.call-update) | async-done | bytes 196624 | tf_op jit(solution)/shard_map/reduce_scatter | solution.py:207
  961.1 22.4 %reduce-scatter.41.cloned.1.call-done = bf16[1,256,384]{1,2,0:T(8,128)(2,1)} async-done(((bf16[1,1024,384]{1,2,0:T(8,128)(2,1)}), bf16[1,256,384]{1,2,0:T(8,128)(2,1)}) %reduce-scatter.41.cloned.1.call-update) | async-done | bytes 196624 | tf_op jit(solution)/shard_map/reduce_scatter | solution.py:207
  988.0 9.8 add_convert_fusion.1
  1025.3 8.9 fusion.132
  1037.3 9.0 fusion.162
  1046.3 8.9 fusion.159
  1071.3 8.0 fusion.153
  1079.3 9.3 fusion.165
  1095.5 41.0 %reduce-scatter.51.cloned.1.call-done = bf16[192,1536]{1,0:T(8,128)(2,1)} async-done(((bf16[768,1536]{1,0:T(8,128)(2,1)}), bf16[192,1536]{1,0:T(8,128)(2,1)}) %reduce-scatter.51.cloned.1.call-update) | async-done | bytes 589840 | tf_op jit(solution)/shard_map/reduce_scatter | solution.py:332
  1136.5 40.4 %reduce-scatter.53.cloned.1.call-done = bf16[1536,192]{0,1:T(8,128)(2,1)} async-done(((bf16[1536,768]{0,1:T(8,128)(2,1)}), bf16[1536,192]{0,1:T(8,128)(2,1)}) %reduce-scatter.53.cloned.1.call-update) | async-done | bytes 589840 | tf_op jit(solution)/shard_map/reduce_scatter | solution.py:335
  1176.9 25.4 %all-reduce.27.cloned.1.call-done = (bf16[256,768]{1,0:T(8,128)(2,1)}, bf16[256,768]{1,0:T(8,128)(2,1)}, bf16[256,768]{1,0:T(8,128)(2,1)}, bf16[256,768]{1,0:T(8...) async-done(((bf16[256,768]{1,0:T(8,128)(2,1)}, bf16[256,768]{1,0:T(8,128)(2,1)}, bf16[256,768]{1,0:T(8,128)(2,1)}, bf16[256,768]{1,0:T(8,128)(2,1)}, ...) | async-done | bytes 2359312 | tf_op jit(solution)/shard_map/psum | solution.py:83
  1206.7 17.5 %all-reduce.7 = (bf16[768]{0:T(1024)(128)(2,1)}, bf16[32,6]{1,0:T(8,128)(2,1)}, bf16[768]{0:T(1024)(128)(2,1)}) all-reduce(bf16[768]{0:T(1024)(128)(2,1)} %add_convert_fusion.3, bf16[32,6]{1,0:T(8,128)(2,1)} %fusion.165, bf16[768]{0:T(1024)(128)(2,1)} %add_convert_fusion.2), channel_id=26, replica_groups=mesh['shard'=4,'context'=4,'tensor'=2] {'shard'}, use_global_device_ids=true, to_apply=%region_84.85.clone | all-reduce | flops 1728 | bytes 6912
  1228.0 13.1 %all-reduce.5 = (bf16[192]{0:T(256)(128)(2,1)}, bf16[8,6]{1,0:T(8,128)(2,1)}, bf16[192]{0:T(256)(128)(2,1)}) all-reduce(bf16[192]{0:T(256)(128)(2,1)} %dynamic-slice.3, bf16[8,6]{1,0:T(8,128)(2,1)} %constant_dynamic-slice_fusion, bf16[192]{0:T(256)(128)(2,1)} %dynamic-slice.7), channel_id=1, replica_groups=mesh['shard'=4,'context'=4,'tensor'=2] {'context'}, use_global_device_ids=true, to_apply=%region_85.86 | all-reduce | flops 432 | bytes 1728 | tf_op jit(solution)/shard_map/psum | solution.py:340
  1251.2 32.9 %all-reduce.25.cloned.1.call-done = (bf16[192,384]{1,0:T(8,128)(2,1)}, bf16[192,384]{1,0:T(8,128)(2,1)}, bf16[192,384]{1,0:T(8,128)(2,1)}, bf16[384,192]{0,1:T(8...) async-done(((bf16[192,384]{1,0:T(8,128)(2,1)}, bf16[192,384]{1,0:T(8,128)(2,1)}, bf16[192,384]{1,0:T(8,128)(2,1)}, bf16[384,192]{0,1:T(8,128)(2,1)}, ...) | async-done | bytes 1769488 | tf_op jit(solution)/shard_map/psum | solution.py:340
  (1018 shorter events, 448.2 us)
Async XLA Ops:
  8.0 36.0 %copy-start.1 = (bf16[3,256,768]{2,1,0:T(8,128)(2,1)S(1)}, bf16[3,256,768]{2,1,0:T(8,128)(2,1)}, u32[]{:S(2)}) copy-start(bf16[3,256,768]{2,1,0:T(8,128)(2,1)} %param.12) | copy-start | bytes 3538948
  8.1 262.9 %all-reduce.39.cloned.1.call-start = ((), (), s32[]{:S(2)}) async-start(), calls=%async_computation.45 | async-start | bytes 2359296 | tf_op jit(solution)/shard_map/psum | solution.py:83
  20.5 349.6 %copy-start.17 = (bf16[768,384]{1,0:T(8,128)(2,1)}, bf16[768,384]{1,0:T(8,128)(2,1)S(1)}, u32[]{:S(2)}) copy-start(bf16[768,384]{1,0:T(8,128)(2,1)S(1)} %all_gather.43) | copy-start | bytes 1769476
  43.4 327.9 %copy-start.14 = (bf16[768,384]{1,0:T(8,128)(2,1)}, bf16[768,384]{1,0:T(8,128)(2,1)S(1)}, u32[]{:S(2)}) copy-start(bf16[768,384]{1,0:T(8,128)(2,1)S(1)} %all_gather.45) | copy-start | bytes 1769476
  57.5 314.8 %copy-start.20 = (bf16[768,384]{1,0:T(8,128)(2,1)}, bf16[768,384]{1,0:T(8,128)(2,1)S(1)}, u32[]{:S(2)}) copy-start(bf16[768,384]{1,0:T(8,128)(2,1)S(1)} %all_gather.46) | copy-start | bytes 1769476
  123.0 512.0 %copy-start.8 = (bf16[384,768]{0,1:T(8,128)(2,1)}, bf16[384,768]{0,1:T(8,128)(2,1)S(1)}, u32[]{:S(2)}) copy-start(bf16[384,768]{0,1:T(8,128)(2,1)S(1)} %all_gather.49) | copy-start | bytes 1769476
  251.9 38.8 %all-gather.15.cloned.1.call-start = ((), (), s32[]{:S(2)}) async-start(), calls=%async_computation.18 | async-start | bytes 2949120 | tf_op jit(solution)/shard_map/all_gather | solution.py:63
  252.5 77.4 %all-gather.17.cloned.1.call-start = ((), (), s32[]{:S(2)}) async-start(), calls=%async_computation.19 | async-start | bytes 2949120 | tf_op jit(solution)/shard_map/all_gather | solution.py:64
  253.0 106.7 %all-reduce.37.cloned.1.call-start = ((), (), s32[]{:S(2)}) async-start(), calls=%async_computation.44 | async-start | bytes 2359296 | tf_op jit(solution)/shard_map/psum | solution.py:83
  339.7 212.4 %all-reduce.35.cloned.1.call-start = ((), (), s32[]{:S(2)}) async-start(), calls=%async_computation.43 | async-start | bytes 2359296 | tf_op jit(solution)/shard_map/psum | solution.py:83
  393.4 30.8 %copy-start.130 = (bf16[1024,384]{0,1:T(8,128)(2,1)}, bf16[1024,384]{0,1:T(8,128)(2,1)S(1)}, u32[]{:S(2)}) copy-start(bf16[1024,384]{0,1:T(8,128)(2,1)S(1)} %copy.128) | copy-start | bytes 2359300
  446.0 30.7 %copy-start.126 = (bf16[1024,384]{0,1:T(8,128)(2,1)}, bf16[1024,384]{0,1:T(8,128)(2,1)S(1)}, u32[]{:S(2)}) copy-start(bf16[1024,384]{0,1:T(8,128)(2,1)S(1)} %copy.122) | copy-start | bytes 2359300
  498.3 29.1 %copy-start.128 = (bf16[1024,384]{0,1:T(8,128)(2,1)}, bf16[1024,384]{0,1:T(8,128)(2,1)S(1)}, u32[]{:S(2)}) copy-start(bf16[1024,384]{0,1:T(8,128)(2,1)S(1)} %copy.116) | copy-start | bytes 2359300
  532.2 62.6 %all-reduce.33.cloned.1.call-start = ((), (), s32[]{:S(2)}) async-start(), calls=%async_computation.42 | async-start | bytes 2359296 | tf_op jit(solution)/shard_map/psum | solution.py:87
  535.2 32.9 %copy-start.292 = (pred[256]{0:T(512)(128)(4,1)}, pred[256]{0:T(512)(128)(4,1)S(1)}, u32[]{:S(2)}) copy-start(pred[256]{0:T(512)(128)(4,1)S(1)} %get-tuple-element.179) | copy-start | bytes 772
  554.2 43.1 %copy-start.23 = (f32[256,768]{1,0:T(8,128)}, f32[256,768]{1,0:T(8,128)S(1)}, u32[]{:S(2)}) copy-start(f32[256,768]{1,0:T(8,128)S(1)} %get-tuple-element.90) | copy-start | bytes 2359300
  555.0 42.3 %copy-start.26 = (f32[256,768]{1,0:T(8,128)}, f32[256,768]{1,0:T(8,128)S(1)}, u32[]{:S(2)}) copy-start(f32[256,768]{1,0:T(8,128)S(1)} %get-tuple-element.88) | copy-start | bytes 2359300
  573.4 85.7 %reduce-scatter.35.cloned.1.call-start = ((), (), s32[]{:S(2)}) async-start(), calls=%async_computation.28 | async-start | bytes 983040 | tf_op jit(solution)/shard_map/reduce_scatter | solution.py:204
  611.0 50.8 %reduce-scatter.37.cloned.1.call-start = ((), (), s32[]{:S(2)}) async-start(), calls=%async_computation.29 | async-start | bytes 983040 | tf_op jit(solution)/shard_map/reduce_scatter | solution.py:207
  616.6 68.7 %reduce-scatter.19.cloned.1.call-start = ((), (), s32[]{:S(2)}) async-start(), calls=%async_computation.20 | async-start | bytes 983040 | tf_op jit(solution)/shard_map/reduce_scatter | solution.py:204
  626.9 83.4 %reduce-scatter.21.cloned.1.call-start = ((), (), s32[]{:S(2)}) async-start(), calls=%async_computation.21 | async-start | bytes 983040 | tf_op jit(solution)/shard_map/reduce_scatter | solution.py:207
  634.9 100.1 %reduce-scatter.27.cloned.1.call-start = ((), (), s32[]{:S(2)}) async-start(), calls=%async_computation.24 | async-start | bytes 983040 | tf_op jit(solution)/shard_map/reduce_scatter | solution.py:204
  645.3 114.5 %reduce-scatter.29.cloned.1.call-start = ((), (), s32[]{:S(2)}) async-start(), calls=%async_computation.25 | async-start | bytes 983040 | tf_op jit(solution)/shard_map/reduce_scatter | solution.py:207
  656.6 125.1 %all-reduce.31.cloned.1.call-start = ((), (), s32[]{:S(2)}) async-start(), calls=%async_computation.41 | async-start | bytes 2359296 | tf_op jit(solution)/shard_map/psum | solution.py:87
  687.5 47.6 %copy-start.133 = (f32[256,768]{1,0:T(8,128)S(1)}, f32[256,768]{1,0:T(8,128)}, u32[]{:S(2)}) copy-start(f32[256,768]{1,0:T(8,128)} %fusion.414) | copy-start | bytes 2359300
  737.3 44.3 %copy-start.45 = (f32[256,768]{1,0:T(8,128)S(1)}, f32[256,768]{1,0:T(8,128)}, u32[]{:S(2)}) copy-start(f32[256,768]{1,0:T(8,128)} %copy-done.43) | copy-start | bytes 2359300
  737.3 44.3 %copy-start.48 = (f32[256,768]{1,0:T(8,128)S(1)}, f32[256,768]{1,0:T(8,128)}, u32[]{:S(2)}) copy-start(f32[256,768]{1,0:T(8,128)} %copy-done.46) | copy-start | bytes 2359300
  737.3 44.3 %copy-start.284 = (f32[256]{0:T(256)S(1)}, f32[256]{0:T(256)}, u32[]{:S(2)}) copy-start(f32[256]{0:T(256)} %copy-done.283) | copy-start | bytes 3076
  737.3 44.3 %copy-start.286 = (f32[256]{0:T(256)S(1)}, f32[256]{0:T(256)}, u32[]{:S(2)}) copy-start(f32[256]{0:T(256)} %copy-done.285) | copy-start | bytes 3076
  762.3 57.9 %all-reduce.29.cloned.1.call-start = ((), (), s32[]{:S(2)}) async-start(), calls=%async_computation.40 | async-start | bytes 2359296 | tf_op jit(solution)/shard_map/psum | solution.py:87
  798.9 112.8 %reduce-scatter.23.cloned.1.call-start = ((), (), s32[]{:S(2)}) async-start(), calls=%async_computation.22 | async-start | bytes 983040 | tf_op jit(solution)/shard_map/reduce_scatter | solution.py:204
  835.1 79.9 %reduce-scatter.31.cloned.1.call-start = ((), (), s32[]{:S(2)}) async-start(), calls=%async_computation.26 | async-start | bytes 983040 | tf_op jit(solution)/shard_map/reduce_scatter | solution.py:204
  848.1 70.2 %reduce-scatter.39.cloned.1.call-start = ((), (), s32[]{:S(2)}) async-start(), calls=%async_computation.30 | async-start | bytes 983040 | tf_op jit(solution)/shard_map/reduce_scatter | solution.py:204
  858.5 75.5 %reduce-scatter.25.cloned.1.call-start = ((), (), s32[]{:S(2)}) async-start(), calls=%async_computation.23 | async-start | bytes 983040 | tf_op jit(solution)/shard_map/reduce_scatter | solution.py:207
  868.4 90.4 %reduce-scatter.33.cloned.1.call-start = ((), (), s32[]{:S(2)}) async-start(), calls=%async_computation.27 | async-start | bytes 983040 | tf_op jit(solution)/shard_map/reduce_scatter | solution.py:207
  882.5 101.0 %reduce-scatter.41.cloned.1.call-start = ((), (), s32[]{:S(2)}) async-start(), calls=%async_computation.31 | async-start | bytes 983040 | tf_op jit(solution)/shard_map/reduce_scatter | solution.py:207
  895.3 193.4 %reduce-scatter.43.cloned.1.call-start = ((), (), s32[]{:S(2)}) async-start(), calls=%async_computation.32 | async-start | bytes 737280 | tf_op jit(solution)/shard_map/reduce_scatter | solution.py:314
  906.0 182.7 %reduce-scatter.49.cloned.1.call-start = ((), (), s32[]{:S(2)}) async-start(), calls=%async_computation.35 | async-start | bytes 737280 | tf_op jit(solution)/shard_map/reduce_scatter | solution.py:323
  911.6 177.1 %reduce-scatter.45.cloned.1.call-start = ((), (), s32[]{:S(2)}) async-start(), calls=%async_computation.33 | async-start | bytes 737280 | tf_op jit(solution)/shard_map/reduce_scatter | solution.py:317
  921.1 174.4 %reduce-scatter.47.cloned.1.call-start = ((), (), s32[]{:S(2)}) async-start(), calls=%async_computation.34 | async-start | bytes 737280 | tf_op jit(solution)/shard_map/reduce_scatter | solution.py:320
  985.8 150.7 %reduce-scatter.51.cloned.1.call-start = ((), (), s32[]{:S(2)}) async-start(), calls=%async_computation.36 | async-start | bytes 2949120 | tf_op jit(solution)/shard_map/reduce_scatter | solution.py:332
  997.8 179.1 %reduce-scatter.53.cloned.1.call-start = ((), (), s32[]{:S(2)}) async-start(), calls=%async_computation.37 | async-start | bytes 2949120 | tf_op jit(solution)/shard_map/reduce_scatter | solution.py:335
  1020.5 181.8 %all-reduce.27.cloned.1.call-start = ((), (), s32[]{:S(2)}) async-start(), calls=%async_computation.39 | async-start | bytes 4718592 | tf_op jit(solution)/shard_map/psum | solution.py:83
  1062.3 221.9 %all-reduce.25.cloned.1.call-start = ((), (), s32[]{:S(2)}) async-start(), calls=%async_computation.38 | async-start | bytes 3538944 | tf_op jit(solution)/shard_map/psum | solution.py:340
  1088.7 113.6 %copy-start.32 = (f32[256,768]{1,0:T(8,128)S(1)}, f32[256,768]{1,0:T(8,128)}, u32[]{:S(2)}) copy-start(f32[256,768]{1,0:T(8,128)} %copy-done.29) | copy-start | bytes 2359300
  1088.7 113.6 %copy-start.299 = (pred[256]{0:T(512)(128)(4,1)S(1)}, pred[256]{0:T(512)(128)(4,1)}, u32[]{:S(2)}) copy-start(pred[256]{0:T(512)(128)(4,1)} %fusion.366) | copy-start | bytes 772
  1204.3 40.6 %copy-start.25 = (f32[256,768]{1,0:T(8,128)S(1)}, f32[256,768]{1,0:T(8,128)}, u32[]{:S(2)}) copy-start(f32[256,768]{1,0:T(8,128)} %copy-done.23) | copy-start | bytes 2359300
  1204.3 41.7 %copy-start.28 = (f32[256,768]{1,0:T(8,128)S(1)}, f32[256,768]{1,0:T(8,128)}, u32[]{:S(2)}) copy-start(f32[256,768]{1,0:T(8,128)} %copy-done.26) | copy-start | bytes 2359300
  (323 other events, 1522.1 us)
Sparse Core Ops, SparseCore 0:
  252.0 18.9 all-reduce.38
  339.8 19.9 all-reduce.36
  532.3 19.7 all-reduce.34
  573.6 21.1 all-reduce.32
  611.1 24.4 reduce-scatter.34
  637.8 22.6 reduce-scatter.36
  662.7 22.4 reduce-scatter.18
  687.6 22.5 reduce-scatter.20
  712.5 22.5 reduce-scatter.26
  737.2 22.5 reduce-scatter.28
  762.4 19.1 all-reduce.30
  799.0 21.1 all-reduce.28
  835.2 24.5 reduce-scatter.22
  861.9 22.5 reduce-scatter.30
  886.7 22.5 reduce-scatter.38
  911.4 22.5 reduce-scatter.24
  936.2 22.5 reduce-scatter.32
  960.9 22.5 reduce-scatter.40
  986.4 24.2 reduce-scatter.42
  1013.6 25.0 reduce-scatter.48
  1041.6 25.0 reduce-scatter.44
  1070.4 25.0 reduce-scatter.46
  1099.1 37.3 reduce-scatter.50
  1139.4 37.4 reduce-scatter.52
  1180.2 22.0 all-reduce.26
  1205.2 78.8 all-reduce.24
Sparse Core Ops, SparseCore 1:
  254.3 36.3 all-gather.14
  292.5 37.3 all-gather.16
where the time goes:
time: 1310 us; the launch traced here: 1300 us
  waiting for transfers between devices  456 us (35%)
  matrix products  360 us (27%)
  blocking collectives  304 us (23%)
  other arithmetic  82.6 us (6%)
  local copies, waits for them, and re-layouts  71.9 us (5%)
  between operations  21.5 us (2%)
    dot_general x151, matrix products, matrix_product(): return jnp.einsum(form, left, right, preferred_element_type=jnp.float32)  360 us
    all_gather x6, blocking collectives, block_forward(): lax.all_gather(values_local.reshape(slots_mb, rows_local, inner_width), '...  111 us
    all_gather x6, blocking collectives, block_forward(): lax.all_gather(keys_local.reshape(slots_mb, rows_local, inner_width), 'co...  103 us
    reduce_scatter x6, waiting for transfers between devices, block_backward(): lax.psum_scatter(value_part.astype(jnp.bfloat16), 'context', scatter_dime...  102 us
    psum x4, waiting for transfers between devices, forward_total(): lax.psum(partial_sum.astype(jnp.bfloat16), 'tensor').astype(jnp.float32)  79.1 us
    psum x3, waiting for transfers between devices, backward_total(): lax.psum(partial_sum.astype(jnp.bfloat16), 'tensor').astype(jnp.float32)  59.2 us
    reduce_scatter x6, waiting for transfers between devices, block_backward(): lax.psum_scatter(key_part.astype(jnp.bfloat16), 'context', scatter_dimens...  43.6 us
    reduce_scatter x1, waiting for transfers between devices, body(): lax.psum_scatter(totals[7].astype(jnp.bfloat16), 'shard', scatter_dimensi...  41 us
  transfers between devices with their start and end apart: 28, of which 20 were waited for; matrix products, arithmetic and copies ran while one was open for 21% of the time, Pallas kernels for 0%

commit v1 on v0

--- a/solution.py
+++ b/solution.py
@@ -84,7 +84,9 @@
 
 
 def backward_total(partial_sum):
-    return lax.psum(partial_sum.astype(jnp.bfloat16), "tensor").astype(jnp.float32)
+    return jnp.sum(lax.all_gather(partial_sum.astype(jnp.bfloat16), "tensor"), axis=0).astype(
+        jnp.float32
+    )
 
 
 def masked_scores(query_heads, key_heads, head_bias_rows, key_valid):

time: 1310 us -> 1260 us (0.962)
  waiting for transfers between devices: 456 us -> 339 us
  blocking collectives: 304 us -> 335 us
  other arithmetic: 82.6 us -> 106 us
  matrix products: 360 us -> 379 us
    psum x3 -> x0, waiting for transfers between devices: 59.2 us -> none  [backward_total(): lax.psum(partial_sum.astype(jnp.bfloat16), 'tensor').astype(jnp.float32)]
    reduce_scatter x6, waiting for transfers between devices: 102 us -> 45.2 us  [block_backward(): lax.psum_scatter(value_part.astype(jnp.bfloat16), 'context', scatter_dime...]
    all_gather x0 -> x12, blocking collectives: none -> 30.8 us  [backward_total(): lax.all_gather(partial_sum.astype(jnp.bfloat16), 'tensor')]
    psum x4, waiting for transfers between devices: 79.1 us -> 48.6 us  [forward_total(): lax.psum(partial_sum.astype(jnp.bfloat16), 'tensor').astype(jnp.float32)]
    reduce_scatter x6, waiting for transfers between devices: 43.6 us -> 71 us  [block_backward(): lax.psum_scatter(key_part.astype(jnp.bfloat16), 'context', scatter_dimens...]
    reduce_sum x0 -> x12, other arithmetic: none -> 19.8 us  [backward_total(): jnp.sum(lax.all_gather(partial_sum.astype(jnp.bfloat16), 'tensor'), axis=0)]
    dot_general x151, matrix products: 360 us -> 379 us  [matrix_product(): return jnp.einsum(form, left, right, preferred_element_type=jnp.float32)]
    unnamed x694 -> x570, local copies, waits for them, and re-layouts: 39.8 us -> 34.6 us
  transfers between devices with their start and end apart: 28 -> 25, of which waited for: 20 -> 16; matrix products, arithmetic and copies ran while one was open for 21% -> 25% of each run, Pallas kernels for 0% -> 0%
where the time goes in v1:
time: 1260 us; the launch traced here: 1250 us
  matrix products  379 us (30%)
  waiting for transfers between devices  339 us (27%)
  blocking collectives  335 us (27%)
  other arithmetic  106 us (8%)
  local copies, waits for them, and re-layouts  70.4 us (6%)
  between operations  20.8 us (2%)
    dot_general x151, matrix products, matrix_product(): return jnp.einsum(form, left, right, preferred_element_type=jnp.float32)  379 us
    all_gather x6, blocking collectives, block_forward(): lax.all_gather(keys_local.reshape(slots_mb, rows_local, inner_width), 'co...  112 us
    all_gather x6, blocking collectives, block_forward(): lax.all_gather(values_local.reshape(slots_mb, rows_local, inner_width), '...  104 us
    reduce_scatter x6, waiting for transfers between devices, block_backward(): lax.psum_scatter(key_part.astype(jnp.bfloat16), 'context', scatter_dimens...  71 us
    psum x4, waiting for transfers between devices, forward_total(): lax.psum(partial_sum.astype(jnp.bfloat16), 'tensor').astype(jnp.float32)  48.6 us
    reduce_scatter x6, waiting for transfers between devices, block_backward(): lax.psum_scatter(value_part.astype(jnp.bfloat16), 'context', scatter_dime...  45.2 us
    reduce_scatter x1, waiting for transfers between devices, body(): lax.psum_scatter(totals[7].astype(jnp.bfloat16), 'shard', scatter_dimensi...  41 us
    reduce_scatter x1, waiting for transfers between devices, body(): lax.psum_scatter(totals[8].astype(jnp.bfloat16), 'shard', scatter_dimensi...  40.5 us
  transfers between devices with their start and end apart: 25, of which 16 were waited for; matrix products, arithmetic and copies ran while one was open for 25% of the time, Pallas kernels for 0%

profile of v1, /device:TPU:0, one launch (start us, length us, event | category | flops | bytes accessed | tf_op | source)
XLA Modules:
  0.0 1253.9 jit_solution(11774075959689847855)
XLA Ops:
  11.9 11.9 all-reduce.8
  25.3 10.4 all_gather.94
  35.7 10.1 all_gather.93
  49.5 9.5 all_gather.91
  64.4 16.9 %all-gather.5 = bf16[1024,384]{1,0:T(8,128)(2,1)} all-gather(bf16[256,384]{1,0:T(8,128)(2,1)S(1)} %convolution_convert_fusion.45), channel_id=7, replica_groups=mesh['shard'=4,'context'=4,'tensor'=2] {'context'}, dimensions={0}, use_global_device_ids=true | all-gather | bytes 983040 | tf_op jit(solution)/shard_map/all_gather | solution.py:111
  86.6 8.2 all_gather.96
  96.1 16.4 %all-gather.4 = bf16[1024,384]{1,0:T(8,128)(2,1)} all-gather(bf16[256,384]{1,0:T(8,128)(2,1)S(1)} %convolution_convert_fusion.47), channel_id=6, replica_groups=mesh['shard'=4,'context'=4,'tensor'=2] {'context'}, dimensions={0}, use_global_device_ids=true | all-gather | bytes 983040 | tf_op jit(solution)/shard_map/all_gather | solution.py:114
  114.8 9.7 all_gather.97
  124.5 20.2 %all-gather.9 = bf16[1024,384]{1,0:T(8,128)(2,1)} all-gather(bf16[256,384]{1,0:T(8,128)(2,1)} %convolution_convert_fusion.39), channel_id=11, replica_groups=mesh['shard'=4,'context'=4,'tensor'=2] {'context'}, dimensions={0}, use_global_device_ids=true | all-gather | bytes 983040 | tf_op jit(solution)/shard_map/all_gather | solution.py:111
  149.4 17.1 %all-gather.8 = bf16[1024,384]{1,0:T(8,128)(2,1)} all-gather(bf16[256,384]{1,0:T(8,128)(2,1)} %convolution_convert_fusion.41), channel_id=10, replica_groups=mesh['shard'=4,'context'=4,'tensor'=2] {'context'}, dimensions={0}, use_global_device_ids=true | all-gather | bytes 983040 | tf_op jit(solution)/shard_map/all_gather | solution.py:114
  168.9 7.0 fusion.6
  196.9 18.7 %all-gather.1 = bf16[1024,384]{1,0:T(8,128)(2,1)} all-gather(bf16[256,384]{1,0:T(8,128)(2,1)S(1)} %copy-done.177), channel_id=3, replica_groups=mesh['shard'=4,'context'=4,'tensor'=2] {'context'}, dimensions={0}, use_global_device_ids=true | all-gather | bytes 983040 | tf_op jit(solution)/shard_map/all_gather | solution.py:111
  220.3 16.8 %all-gather = bf16[1024,384]{1,0:T(8,128)(2,1)} all-gather(bf16[256,384]{1,0:T(8,128)(2,1)} %convolution_convert_fusion.53), channel_id=2, replica_groups=mesh['shard'=4,'context'=4,'tensor'=2] {'context'}, dimensions={0}, use_global_device_ids=true | all-gather | bytes 983040 | tf_op jit(solution)/shard_map/all_gather | solution.py:114
  239.5 8.2 fusion.407
  256.3 16.9 %all-reduce.27.cloned.1.call-done = (bf16[256,768]{1,0:T(8,128)(2,1)}, bf16[256,768]{1,0:T(8,128)(2,1)}, bf16[256,768]{1,0:T(8,128)(2,1)}) async-done(((bf16[256,768]{1,0:T(8,128)(2,1)}, bf16[256,768]{1,0:T(8,128)(2,1)}, bf16[256,768]{1,0:T(8,128)(2,1)}), (bf16[256,768]{1,0:T(8,128)(2,1)}, bf16[256,768]{1,0:T(8,128)(2,1)}, bf16[256,768]{1,0:T(8,128)(2,1)})) %all-reduce.27.cloned.1.call-update) | async-done | bytes 1179664 | tf_op jit(solution)/shard_map/psum | solution.py:83
  276.7 16.1 %all-gather.27.cloned.1.call-done = bf16[768,1536]{1,0:T(8,128)(2,1)} async-done(((bf16[192,1536]{1,0:T(8,128)(2,1)}), bf16[768,1536]{1,0:T(8,128)(2,1)}) %all-gather.27.cloned.1.call-update) | async-done | bytes 2359312 | tf_op jit(solution)/shard_map/all_gather | solution.py:63
  298.8 33.3 %all-gather.29.cloned.1.call-done = bf16[1536,768]{0,1:T(8,128)(2,1)} async-done(((bf16[1536,192]{0,1:T(8,128)(2,1)}), bf16[1536,768]{0,1:T(8,128)(2,1)}) %all-gather.29.cloned.1.call-update) | async-done | bytes 2359312 | tf_op jit(solution)/shard_map/all_gather | solution.py:64
  346.4 15.6 %all-reduce.25.cloned.1.call-done = (bf16[256,768]{1,0:T(8,128)(2,1)}, bf16[256,768]{1,0:T(8,128)(2,1)}, bf16[256,768]{1,0:T(8,128)(2,1)}) async-done(((bf16[256,768]{1,0:T(8,128)(2,1)}, bf16[256,768]{1,0:T(8,128)(2,1)}, bf16[256,768]{1,0:T(8,128)(2,1)}), (bf16[256,768]{1,0:T(8,128)(2,1)}, bf16[256,768]{1,0:T(8,128)(2,1)}, bf16[256,768]{1,0:T(8,128)(2,1)})) %all-reduce.25.cloned.1.call-update) | async-done | bytes 1179664 | tf_op jit(solution)/shard_map/psum | solution.py:83
  374.8 19.8 %all-gather.11 = bf16[1024,384]{1,0:T(8,128)(2,1)S(1)} all-gather(bf16[256,384]{1,0:T(8,128)(2,1)S(1)} %convolution_convert_fusion.36), channel_id=13, replica_groups=mesh['shard'=4,'context'=4,'tensor'=2] {'context'}, dimensions={0}, use_global_device_ids=true | all-gather | bytes 983040 | tf_op jit(solution)/shard_map/all_gather | solution.py:111
  396.0 18.2 %all-gather.3 = bf16[1024,384]{1,0:T(8,128)(2,1)} all-gather(bf16[256,384]{1,0:T(8,128)(2,1)} %convolution_convert_fusion.48), channel_id=5, replica_groups=mesh['shard'=4,'context'=4,'tensor'=2] {'context'}, dimensions={0}, use_global_device_ids=true | all-gather | bytes 983040 | tf_op jit(solution)/shard_map/all_gather | solution.py:111
  416.9 18.5 %all-gather.2 = bf16[1024,384]{1,0:T(8,128)(2,1)} all-gather(bf16[256,384]{1,0:T(8,128)(2,1)} %convolution_convert_fusion.50), channel_id=4, replica_groups=mesh['shard'=4,'context'=4,'tensor'=2] {'context'}, dimensions={0}, use_global_device_ids=true | all-gather | bytes 983040 | tf_op jit(solution)/shard_map/all_gather | solution.py:114
  437.7 7.9 fusion.411
  451.2 17.9 %all-gather.7 = bf16[1024,384]{1,0:T(8,128)(2,1)} all-gather(bf16[256,384]{1,0:T(8,128)(2,1)S(1)} %copy-done.158), channel_id=9, replica_groups=mesh['shard'=4,'context'=4,'tensor'=2] {'context'}, dimensions={0}, use_global_device_ids=true | all-gather | bytes 983040 | tf_op jit(solution)/shard_map/all_gather | solution.py:111
  471.7 17.8 %all-gather.6 = bf16[1024,384]{1,0:T(8,128)(2,1)} all-gather(bf16[256,384]{1,0:T(8,128)(2,1)} %convolution_convert_fusion.44), channel_id=8, replica_groups=mesh['shard'=4,'context'=4,'tensor'=2] {'context'}, dimensions={0}, use_global_device_ids=true | all-gather | bytes 983040 | tf_op jit(solution)/shard_map/all_gather | solution.py:114
  491.8 7.9 fusion.410
  505.9 16.9 %all-gather.10 = bf16[1024,384]{1,0:T(8,128)(2,1)} all-gather(bf16[256,384]{1,0:T(8,128)(2,1)S(1)} %copy-done.157), channel_id=12, replica_groups=mesh['shard'=4,'context'=4,'tensor'=2] {'context'}, dimensions={0}, use_global_device_ids=true | all-gather | bytes 983040 | tf_op jit(solution)/shard_map/all_gather | solution.py:114
  525.1 7.9 fusion.409
  543.3 16.1 %all-reduce.23.cloned.1.call-done = (bf16[256,768]{1,0:T(8,128)(2,1)}, bf16[256,768]{1,0:T(8,128)(2,1)}, bf16[256,768]{1,0:T(8,128)(2,1)}) async-done(((bf16[256,768]{1,0:T(8,128)(2,1)}, bf16[256,768]{1,0:T(8,128)(2,1)}, bf16[256,768]{1,0:T(8,128)(2,1)}), (bf16[256,768]{1,0:T(8,128)(2,1)}, bf16[256,768]{1,0:T(8,128)(2,1)}, bf16[256,768]{1,0:T(8,128)(2,1)})) %all-reduce.23.cloned.1.call-update) | async-done | bytes 1179664 | tf_op jit(solution)/shard_map/psum | solution.py:83
  689.4 6.5 reduce-scatter.19.cloned.1.call-done
  698.1 22.7 %reduce-scatter.21.cloned.1.call-done = bf16[1,256,384]{1,2,0:T(8,128)(2,1)} async-done(((bf16[1,1024,384]{1,2,0:T(8,128)(2,1)}), bf16[1,256,384]{1,2,0:T(8,128)(2,1)}) %reduce-scatter.21.cloned.1.call-update) | async-done | bytes 196624 | tf_op jit(solution)/shard_map/reduce_scatter | solution.py:209
  724.9 21.3 %reduce-scatter.27.cloned.1.call-done = bf16[1,256,384]{1,2,0:T(8,128)(2,1)} async-done(((bf16[1,1024,384]{1,2,0:T(8,128)(2,1)}), bf16[1,256,384]{1,2,0:T(8,128)(2,1)}) %reduce-scatter.27.cloned.1.call-update) | async-done | bytes 196624 | tf_op jit(solution)/shard_map/reduce_scatter | solution.py:206
  748.5 22.5 %reduce-scatter.29.cloned.1.call-done = bf16[1,256,384]{1,2,0:T(8,128)(2,1)} async-done(((bf16[1,1024,384]{1,2,0:T(8,128)(2,1)}), bf16[1,256,384]{1,2,0:T(8,128)(2,1)}) %reduce-scatter.29.cloned.1.call-update) | async-done | bytes 196624 | tf_op jit(solution)/shard_map/reduce_scatter | solution.py:209
  920.9 21.4 %reduce-scatter.31.cloned.1.call-done = bf16[1,256,384]{1,2,0:T(8,128)(2,1)} async-done(((bf16[1,1024,384]{1,2,0:T(8,128)(2,1)}), bf16[1,256,384]{1,2,0:T(8,128)(2,1)}) %reduce-scatter.31.cloned.1.call-update) | async-done | bytes 196624 | tf_op jit(solution)/shard_map/reduce_scatter | solution.py:206
  945.6 21.4 %reduce-scatter.39.cloned.1.call-done = bf16[1,256,384]{1,2,0:T(8,128)(2,1)} async-done(((bf16[1,1024,384]{1,2,0:T(8,128)(2,1)}), bf16[1,256,384]{1,2,0:T(8,128)(2,1)}) %reduce-scatter.39.cloned.1.call-update) | async-done | bytes 196624 | tf_op jit(solution)/shard_map/reduce_scatter | solution.py:206
  972.5 9.2 add_convert_fusion
  982.0 8.3 fusion.132
  1000.4 8.1 fusion.162
  1008.5 7.9 fusion.159
  1016.4 11.0 add_convert_fusion.1
  1028.8 7.8 fusion.156
  1036.6 8.0 fusion.153
  1044.7 9.4 fusion.165
  1070.4 7.7 reduce-scatter.45.cloned.1.call-done
  1078.2 40.5 %reduce-scatter.53.cloned.1.call-done = bf16[1536,192]{0,1:T(8,128)(2,1)} async-done(((bf16[1536,768]{0,1:T(8,128)(2,1)}), bf16[1536,192]{0,1:T(8,128)(2,1)}) %reduce-scatter.53.cloned.1.call-update) | async-done | bytes 589840 | tf_op jit(solution)/shard_map/reduce_scatter | solution.py:337
  1118.6 41.0 %reduce-scatter.51.cloned.1.call-done = bf16[192,1536]{1,0:T(8,128)(2,1)} async-done(((bf16[768,1536]{1,0:T(8,128)(2,1)}), bf16[192,1536]{1,0:T(8,128)(2,1)}) %reduce-scatter.51.cloned.1.call-update) | async-done | bytes 589840 | tf_op jit(solution)/shard_map/reduce_scatter | solution.py:334
  1163.5 16.3 %all-reduce.7 = (bf16[768]{0:T(1024)(128)(2,1)}, bf16[32,6]{1,0:T(8,128)(2,1)}, bf16[768]{0:T(1024)(128)(2,1)}) all-reduce(bf16[768]{0:T(1024)(128)(2,1)} %add_convert_fusion.3, bf16[32,6]{1,0:T(8,128)(2,1)} %fusion.165, bf16[768]{0:T(1024)(128)(2,1)} %add_convert_fusion.2), channel_id=38, replica_groups=mesh['shard'=4,'context'=4,'tensor'=2] {'shard'}, use_global_device_ids=true, to_apply=%region_84.85.clone | all-reduce | flops 1728 | bytes 6912
  1183.5 13.2 %all-reduce.5 = (bf16[192]{0:T(256)(128)(2,1)}, bf16[8,6]{1,0:T(8,128)(2,1)}, bf16[192]{0:T(256)(128)(2,1)}) all-reduce(bf16[192]{0:T(256)(128)(2,1)} %dynamic-slice.3, bf16[8,6]{1,0:T(8,128)(2,1)} %constant_dynamic-slice_fusion, bf16[192]{0:T(256)(128)(2,1)} %dynamic-slice.7), channel_id=1, replica_groups=mesh['shard'=4,'context'=4,'tensor'=2] {'context'}, use_global_device_ids=true, to_apply=%region_85.86 | all-reduce | flops 432 | bytes 1728 | tf_op jit(solution)/shard_map/psum | solution.py:342
  1206.0 34.3 %all-reduce.19.cloned.1.call-done = (bf16[192,384]{1,0:T(8,128)(2,1)}, bf16[192,384]{1,0:T(8,128)(2,1)}, bf16[192,384]{1,0:T(8,128)(2,1)}, bf16[384,192]{0,1:T(8...) async-done(((bf16[192,384]{1,0:T(8,128)(2,1)}, bf16[192,384]{1,0:T(8,128)(2,1)}, bf16[192,384]{1,0:T(8,128)(2,1)}, bf16[384,192]{0,1:T(8,128)(2,1)}, ...) | async-done | bytes 1769488 | tf_op jit(solution)/shard_map/psum | solution.py:342
  (905 shorter events, 482.5 us)
Async XLA Ops:
  8.0 38.4 %copy-start.1 = (bf16[3,256,768]{2,1,0:T(8,128)(2,1)S(1)}, bf16[3,256,768]{2,1,0:T(8,128)(2,1)}, u32[]{:S(2)}) copy-start(bf16[3,256,768]{2,1,0:T(8,128)(2,1)} %param.12) | copy-start | bytes 3538948
  8.0 27.7 %copy-start.183 = (bf16[192,384]{1,0:T(8,128)(2,1)S(1)}, bf16[192,384]{1,0:T(8,128)(2,1)}, u32[]{:S(2)}) copy-start(bf16[192,384]{1,0:T(8,128)(2,1)} %param.16) | copy-start | bytes 442372
  8.0 265.3 %all-reduce.27.cloned.1.call-start = ((), (), s32[]{:S(2)}) async-start(), calls=%async_computation.42 | async-start | bytes 2359296 | tf_op jit(solution)/shard_map/psum | solution.py:83
  35.7 710.5 %copy-start.14 = (bf16[768,384]{1,0:T(8,128)(2,1)}, bf16[768,384]{1,0:T(8,128)(2,1)S(1)}, u32[]{:S(2)}) copy-start(bf16[768,384]{1,0:T(8,128)(2,1)S(1)} %all_gather.94) | copy-start | bytes 1769476
  46.4 12.6 %copy-start.216 = (f32[256]{0:T(256)}, f32[256]{0:T(256)S(1)}, u32[]{:S(2)}) copy-start(f32[256]{0:T(256)S(1)} %get-tuple-element.169) | copy-start | bytes 3076
  46.4 13.1 %copy-start.214 = (f32[256]{0:T(256)}, f32[256]{0:T(256)S(1)}, u32[]{:S(2)}) copy-start(f32[256]{0:T(256)S(1)} %get-tuple-element.121) | copy-start | bytes 3076
  59.0 712.0 %copy-start.16 = (bf16[768,384]{1,0:T(8,128)(2,1)}, bf16[768,384]{1,0:T(8,128)(2,1)S(1)}, u32[]{:S(2)}) copy-start(bf16[768,384]{1,0:T(8,128)(2,1)S(1)} %all_gather.91) | copy-start | bytes 1769476
  81.4 13.4 %copy-start.248 = (s32[3]{0:T(128)S(1)}, s32[3]{0:T(128)}, u32[]{:S(2)}) copy-start(s32[3]{0:T(128)} %param.13) | copy-start | bytes 40
  220.3 27.4 %copy-start.178 = (pred[1024]{0:T(1024)(128)(4,1)}, pred[1024]{0:T(1024)(128)(4,1)S(1)}, u32[]{:S(2)}) copy-start(pred[1024]{0:T(1024)(128)(4,1)S(1)} %iota_compare_fusion.34) | copy-start | bytes 3076
  254.0 38.9 %all-gather.27.cloned.1.call-start = ((), (), s32[]{:S(2)}) async-start(), calls=%async_computation.18 | async-start | bytes 2949120 | tf_op jit(solution)/shard_map/all_gather | solution.py:63
  254.6 77.5 %all-gather.29.cloned.1.call-start = ((), (), s32[]{:S(2)}) async-start(), calls=%async_computation.19 | async-start | bytes 2949120 | tf_op jit(solution)/shard_map/all_gather | solution.py:64
  255.1 106.9 %all-reduce.25.cloned.1.call-start = ((), (), s32[]{:S(2)}) async-start(), calls=%async_computation.41 | async-start | bytes 2359296 | tf_op jit(solution)/shard_map/psum | solution.py:83
  341.9 217.6 %all-reduce.23.cloned.1.call-start = ((), (), s32[]{:S(2)}) async-start(), calls=%async_computation.40 | async-start | bytes 2359296 | tf_op jit(solution)/shard_map/psum | solution.py:83
  396.0 129.1 %copy-start.133 = (bf16[256,384]{0,1:T(8,128)(2,1)}, bf16[256,384]{0,1:T(8,128)(2,1)S(1)}, u32[]{:S(2)}) copy-start(bf16[256,384]{0,1:T(8,128)(2,1)S(1)} %copy.129) | copy-start | bytes 589828
  415.6 30.1 %copy-start.87 = (bf16[1024,384]{0,1:T(8,128)(2,1)}, bf16[1024,384]{0,1:T(8,128)(2,1)S(1)}, u32[]{:S(2)}) copy-start(bf16[1024,384]{0,1:T(8,128)(2,1)S(1)} %copy.118) | copy-start | bytes 2359300
  416.9 28.8 %copy-start.131 = (bf16[256,384]{0,1:T(8,128)(2,1)}, bf16[256,384]{0,1:T(8,128)(2,1)S(1)}, u32[]{:S(2)}) copy-start(bf16[256,384]{0,1:T(8,128)(2,1)S(1)} %copy.117) | copy-start | bytes 589828
  470.4 29.3 %copy-start.89 = (bf16[1024,384]{0,1:T(8,128)(2,1)}, bf16[1024,384]{0,1:T(8,128)(2,1)S(1)}, u32[]{:S(2)}) copy-start(bf16[1024,384]{0,1:T(8,128)(2,1)S(1)} %copy.124) | copy-start | bytes 2359300
  471.7 28.0 %copy-start.129 = (bf16[256,384]{0,1:T(8,128)(2,1)}, bf16[256,384]{0,1:T(8,128)(2,1)S(1)}, u32[]{:S(2)}) copy-start(bf16[256,384]{0,1:T(8,128)(2,1)S(1)} %copy.123) | copy-start | bytes 589828
  505.9 19.2 %copy-start.91 = (bf16[1024,384]{0,1:T(8,128)(2,1)S(1)}, bf16[1024,384]{0,1:T(8,128)(2,1)}, u32[]{:S(2)}) copy-start(bf16[1024,384]{0,1:T(8,128)(2,1)} %copy.130) | copy-start | bytes 2359300
  539.2 66.4 %all-reduce.21.cloned.1.call-start = ((), (), s32[]{:S(2)}) async-start(), calls=%async_computation.39 | async-start | bytes 2359296 | tf_op jit(solution)/shard_map/psum | solution.py:83
  561.0 44.6 %copy-start.28 = (f32[256,768]{1,0:T(8,128)}, f32[256,768]{1,0:T(8,128)S(1)}, u32[]{:S(2)}) copy-start(f32[256,768]{1,0:T(8,128)S(1)} %get-tuple-element.80) | copy-start | bytes 2359300
  574.7 108.3 %reduce-scatter.35.cloned.1.call-start = ((), (), s32[]{:S(2)}) async-start(), calls=%async_computation.28 | async-start | bytes 983040 | tf_op jit(solution)/shard_map/reduce_scatter | solution.py:206
  621.5 63.7 %reduce-scatter.37.cloned.1.call-start = ((), (), s32[]{:S(2)}) async-start(), calls=%async_computation.29 | async-start | bytes 983040 | tf_op jit(solution)/shard_map/reduce_scatter | solution.py:209
  633.5 62.4 %reduce-scatter.19.cloned.1.call-start = ((), (), s32[]{:S(2)}) async-start(), calls=%async_computation.20 | async-start | bytes 983040 | tf_op jit(solution)/shard_map/reduce_scatter | solution.py:206
  647.1 73.7 %reduce-scatter.21.cloned.1.call-start = ((), (), s32[]{:S(2)}) async-start(), calls=%async_computation.21 | async-start | bytes 983040 | tf_op jit(solution)/shard_map/reduce_scatter | solution.py:209
  647.3 11.0 slice-start.10
  660.4 85.8 %reduce-scatter.27.cloned.1.call-start = ((), (), s32[]{:S(2)}) async-start(), calls=%async_computation.24 | async-start | bytes 983040 | tf_op jit(solution)/shard_map/reduce_scatter | solution.py:206
  671.0 100.0 %reduce-scatter.29.cloned.1.call-start = ((), (), s32[]{:S(2)}) async-start(), calls=%async_computation.25 | async-start | bytes 983040 | tf_op jit(solution)/shard_map/reduce_scatter | solution.py:209
  682.9 224.7 %reduce-scatter.25.cloned.1.call-start = ((), (), s32[]{:S(2)}) async-start(), calls=%async_computation.23 | async-start | bytes 983040 | tf_op jit(solution)/shard_map/reduce_scatter | solution.py:209
  698.1 48.1 %copy-start.116 = (f32[256,768]{1,0:T(8,128)S(1)}, f32[256,768]{1,0:T(8,128)}, u32[]{:S(2)}) copy-start(f32[256,768]{1,0:T(8,128)} %fusion.414) | copy-start | bytes 2359300
  784.1 12.7 %copy-start.93 = (f32[256,768]{1,0:T(8,128)}, f32[256,768]{1,0:T(8,128)S(1)}, u32[]{:S(2)}) copy-start(f32[256,768]{1,0:T(8,128)S(1)} %get-tuple-element.102) | copy-start | bytes 2359300
  820.3 90.7 %reduce-scatter.33.cloned.1.call-start = ((), (), s32[]{:S(2)}) async-start(), calls=%async_computation.27 | async-start | bytes 983040 | tf_op jit(solution)/shard_map/reduce_scatter | solution.py:209
  837.0 77.4 %reduce-scatter.41.cloned.1.call-start = ((), (), s32[]{:S(2)}) async-start(), calls=%async_computation.31 | async-start | bytes 983040 | tf_op jit(solution)/shard_map/reduce_scatter | solution.py:209
  848.7 68.8 %reduce-scatter.23.cloned.1.call-start = ((), (), s32[]{:S(2)}) async-start(), calls=%async_computation.22 | async-start | bytes 983040 | tf_op jit(solution)/shard_map/reduce_scatter | solution.py:206
  859.8 82.4 %reduce-scatter.31.cloned.1.call-start = ((), (), s32[]{:S(2)}) async-start(), calls=%async_computation.26 | async-start | bytes 983040 | tf_op jit(solution)/shard_map/reduce_scatter | solution.py:206
  870.7 96.4 %reduce-scatter.39.cloned.1.call-start = ((), (), s32[]{:S(2)}) async-start(), calls=%async_computation.30 | async-start | bytes 983040 | tf_op jit(solution)/shard_map/reduce_scatter | solution.py:206
  881.7 188.8 %reduce-scatter.49.cloned.1.call-start = ((), (), s32[]{:S(2)}) async-start(), calls=%async_computation.35 | async-start | bytes 737280 | tf_op jit(solution)/shard_map/reduce_scatter | solution.py:325
  892.7 177.7 %reduce-scatter.43.cloned.1.call-start = ((), (), s32[]{:S(2)}) async-start(), calls=%async_computation.32 | async-start | bytes 737280 | tf_op jit(solution)/shard_map/reduce_scatter | solution.py:316
  903.8 166.7 %reduce-scatter.47.cloned.1.call-start = ((), (), s32[]{:S(2)}) async-start(), calls=%async_computation.34 | async-start | bytes 737280 | tf_op jit(solution)/shard_map/reduce_scatter | solution.py:322
  917.1 161.0 %reduce-scatter.45.cloned.1.call-start = ((), (), s32[]{:S(2)}) async-start(), calls=%async_computation.33 | async-start | bytes 737280 | tf_op jit(solution)/shard_map/reduce_scatter | solution.py:319
  920.9 23.3 %copy-start.152 = (bf16[1,256,384]{1,2,0:T(8,128)(2,1)S(1)}, bf16[1,256,384]{1,2,0:T(8,128)(2,1)}, u32[]{:S(2)}) copy-start(bf16[1,256,384]{1,2,0:T(8,128)(2,1)} %reduce-scatter.35.cloned.1.call-done) | copy-start | bytes 589828
  969.8 148.9 %reduce-scatter.53.cloned.1.call-start = ((), (), s32[]{:S(2)}) async-start(), calls=%async_computation.37 | async-start | bytes 2949120 | tf_op jit(solution)/shard_map/reduce_scatter | solution.py:337
  981.8 177.9 %reduce-scatter.51.cloned.1.call-start = ((), (), s32[]{:S(2)}) async-start(), calls=%async_computation.36 | async-start | bytes 2949120 | tf_op jit(solution)/shard_map/reduce_scatter | solution.py:334
  1027.5 212.7 %all-reduce.19.cloned.1.call-start = ((), (), s32[]{:S(2)}) async-start(), calls=%async_computation.38 | async-start | bytes 3538944 | tf_op jit(solution)/shard_map/psum | solution.py:342
  1069.4 90.3 %copy-start.219 = (f32[256]{0:T(256)S(1)}, f32[256]{0:T(256)}, u32[]{:S(2)}) copy-start(f32[256]{0:T(256)} %copy-done.216) | copy-start | bytes 3076
  1159.7 42.7 %copy-start.61 = (f32[256,768]{1,0:T(8,128)S(1)}, f32[256,768]{1,0:T(8,128)}, u32[]{:S(2)}) copy-start(f32[256,768]{1,0:T(8,128)} %get-tuple-element.90) | copy-start | bytes 2359300
  1159.7 42.7 %copy-start.63 = (f32[256,768]{1,0:T(8,128)S(1)}, f32[256,768]{1,0:T(8,128)}, u32[]{:S(2)}) copy-start(f32[256,768]{1,0:T(8,128)} %copy-done.62) | copy-start | bytes 2359300
  1159.8 42.7 %copy-start.66 = (f32[256,768]{1,0:T(8,128)S(1)}, f32[256,768]{1,0:T(8,128)}, u32[]{:S(2)}) copy-start(f32[256,768]{1,0:T(8,128)} %copy-done.64) | copy-start | bytes 2359300
  (258 other events, 840.8 us)
Sparse Core Ops, SparseCore 0:
  254.1 19.1 all-reduce.26
  342.0 19.9 all-reduce.24
  539.3 20.1 all-reduce.22
  574.8 21.1 all-reduce.20
  621.6 24.5 reduce-scatter.34
  648.4 22.5 reduce-scatter.36
  673.3 22.5 reduce-scatter.18
  698.2 22.5 reduce-scatter.20
  723.7 22.5 reduce-scatter.26
  748.4 22.5 reduce-scatter.28
  820.4 22.5 reduce-scatter.24
  845.2 22.5 reduce-scatter.32
  870.2 22.5 reduce-scatter.40
  895.0 22.5 reduce-scatter.22
  919.7 22.5 reduce-scatter.30
  944.4 22.5 reduce-scatter.38
  969.7 24.2 reduce-scatter.48
  997.0 25.0 reduce-scatter.42
  1025.0 25.0 reduce-scatter.46
  1053.0 25.0 reduce-scatter.44
  1081.2 37.3 reduce-scatter.52
  1122.2 37.3 reduce-scatter.50
  1162.5 77.6 all-reduce.18
Sparse Core Ops, SparseCore 1:
  256.3 36.5 all-gather.26
  294.7 37.3 all-gather.28
